TPU v7x, 256 devices: a whole 4x4x8 slice. The times are simulated.
256 devices in a mesh: grp: 64 (over z, y, core), head: 4 (over x).
Axes of the slice: x: 4, y: 4, z: 8, core: 2. Of those that a mesh axis runs over, the one named last changes fastest.
Arguments:
- arriving_hiddens: bfloat16 [512, 4, 2048], P('grp', None, 'head'), may hold values from -6 to 6
- occupied_slot_totals: int32 [512], P('grp'), may hold values from 1 to 4
- former_indices: int32 [512], P('grp'), may hold values from 0 to 511, as said below
- reconstruct_marks: int32 [512], P('grp'), may hold values from 0 to 1, as said below
- retained_hiddens: bfloat16 [512, 32, 2048], P('grp', None, 'head'), may hold values from -6 to 6
- carried_memory_matrices: float32 [512, 16, 64, 64], P('grp', 'head'), may hold values from -12 to 12
- lagged_previous_entries: float32 [512, 2, 2048], P('grp', None, 'head'), may hold values from -6 to 6
- pre_attention_scaling: float32 [2048], replicated, may hold values from 0.5 to 1.5
- pre_feedforward_scaling: float32 [2048], replicated, may hold values from 0.5 to 1.5
- lag_blend_fractions: float32 [5, 2048], replicated, may hold values from 0 to 1
- acceptance_projection: bfloat16 [2048, 1024], P(None, 'head'), may hold values from -0.125 to 0.125
- address_projection: bfloat16 [2048, 1024], P(None, 'head'), may hold values from -0.125 to 0.125
- content_projection: bfloat16 [2048, 1024], P(None, 'head'), may hold values from -0.125 to 0.125
- fading_lowrank_left: bfloat16 [2048, 64], replicated, may hold values from -0.125 to 0.125
- fading_lowrank_right: bfloat16 [64, 1024], P(None, 'head'), may hold values from -0.75 to 0.75
- fading_baseline_entries: float32 [1024], P('head'), may hold values from -6 to 1
- present_item_reward: float32 [1024], P('head'), may hold values from -6 to 6
- grouped_layer_scaling: float32 [1024], P('head'), may hold values from 0.5 to 1.5
- attention_exit_projection: bfloat16 [1024, 2048], P('head'), may hold values from -0.1875 to 0.1875
- feedforward_address_proj: bfloat16 [2048, 3584], P(None, 'head'), may hold values from -0.125 to 0.125
- feedforward_content_proj: bfloat16 [3584, 2048], P('head'), may hold values from -0.09375 to 0.09375
Outputs:
- next_tokens: bfloat16 [512, 4, 2048], P('grp', None, 'head')
- next_state: float32 [512, 16, 64, 64], P('grp', 'head')
- next_shift: float32 [512, 2, 2048], P('grp', None, 'head')
Inputs may be any that keep to these rules, and one draw needn't show every extreme that they name: former_indices[g * 8 + j] = ((g + offset_j) mod 64) * 8 + local_j, where the 8 offsets offset_j are distinct numbers of 0 to 63 and local_j is a permutation of 0 to 7, both the same for every group g. `reconstruct_marks`: among the 8 requests of one group at most 2 are marked, and some group has exactly 2.
All inputs are finite; a program needn't handle non-finite values.
Results may differ from a plain program's by a relative error of at most 0.028.
Values may be sent and summed in bfloat16 or wider, within the bound.
No kernel may reach another device: no remote copies, remote signals or barrier semaphores. Data moves between devices by JAX's collectives and lax.ppermute only.
A program may use at most 128 MiB of HBM per device.

v0:
```python
import jax
import jax.numpy as jnp
from jax import lax
from jax.sharding import PartitionSpec as P

ATTENTION_WIDTH = 64
REB = 2
EPSILON = 1e-05


def shifted_2(value, axis, steps):
    count = lax.axis_size(axis)
    pairs = [(source, (source + steps) % count) for source in range(count)]
    return lax.ppermute(value, axis, pairs)


def layer_norm(inputs, gain):
    centered = inputs - jnp.mean(inputs, axis=-1, keepdims=True)
    spread = jnp.mean(centered * centered, axis=-1, keepdims=True)
    return (centered * lax.rsqrt(spread + EPSILON) * gain).astype(jnp.bfloat16)


def blend_rows(current, previous, rate):
    return (current + (previous - current) * rate).astype(jnp.bfloat16)


def project(inputs, weight):
    flat_rows = inputs.reshape(-1, inputs.shape[-1])
    result = jnp.dot(flat_rows, weight, preferred_element_type=jnp.float32)
    return result.reshape(inputs.shape[:-1] + (weight.shape[1],))


def divide_into_groups(inputs):
    return inputs.reshape(inputs.shape[:-1] + (-1, ATTENTION_WIDTH))


def key_value_decay(
    current,
    previous,
    lag_blend_fractions,
    address_projection,
    content_projection,
    fading_lowrank_left,
    fading_lowrank_right,
    fading_baseline_entries,
):
    key_rows = project(blend_rows(current, previous, lag_blend_fractions[1]), address_projection)
    values = project(blend_rows(current, previous, lag_blend_fractions[2]), content_projection)
    lowrank = jnp.tanh(
        project(blend_rows(current, previous, lag_blend_fractions[3]), fading_lowrank_left)
    ).astype(jnp.bfloat16)
    decay_rates = jnp.exp(
        -jnp.exp(fading_baseline_entries + project(lowrank, fading_lowrank_right))
    )
    return (
        divide_into_groups(key_rows),
        divide_into_groups(values),
        divide_into_groups(decay_rates),
    )


def advance(present_outer_product, inputs):
    key_step, value_step, decay_step = inputs
    return (
        decay_step[..., :, None] * present_outer_product
        + key_step[..., :, None] * value_step[..., None, :],
        None,
    )


def rebuild(
    retained_hiddens,
    pre_attention_scaling,
    lag_blend_fractions,
    address_projection,
    content_projection,
    fading_lowrank_left,
    fading_lowrank_right,
    fading_baseline_entries,
):
    standardized_entry = layer_norm(retained_hiddens.astype(jnp.float32), pre_attention_scaling)
    current = standardized_entry.astype(jnp.float32)
    previous = jnp.concatenate([jnp.zeros_like(current[:, :1]), current[:, :-1]], axis=1)
    key_rows, values, decay_rates = key_value_decay(
        current,
        previous,
        lag_blend_fractions,
        address_projection,
        content_projection,
        fading_lowrank_left,
        fading_lowrank_right,
        fading_baseline_entries,
    )
    start_state = jnp.zeros(
        key_rows.shape[:1] + key_rows.shape[2:] + (ATTENTION_WIDTH,), jnp.float32
    )
    final_state, _ = lax.scan(
        advance,
        start_state,
        (jnp.moveaxis(key_rows, 1, 0), jnp.moveaxis(values, 1, 0), jnp.moveaxis(decay_rates, 1, 0)),
    )
    return (final_state, current[:, -1])


def attention_result(
    standardized_entry,
    lagged_entry,
    present_outer_product,
    occupied_slot_totals,
    lag_blend_fractions,
    acceptance_projection,
    address_projection,
    content_projection,
    fading_lowrank_left,
    fading_lowrank_right,
    fading_baseline_entries,
    present_item_reward,
    grouped_layer_scaling,
):
    current = standardized_entry.astype(jnp.float32)
    previous = jnp.concatenate([lagged_entry[:, None], current[:, :-1]], axis=1)
    acceptance_gate_entries = divide_into_groups(
        project(blend_rows(current, previous, lag_blend_fractions[0]), acceptance_projection)
    )
    key_rows, values, decay_rates = key_value_decay(
        current,
        previous,
        lag_blend_fractions,
        address_projection,
        content_projection,
        fading_lowrank_left,
        fading_lowrank_right,
        fading_baseline_entries,
    )
    reward_grouped = divide_into_groups(present_item_reward)
    decoding_results = []
    for query_slot_index in range(current.shape[1]):
        address_content_product = (
            key_rows[:, query_slot_index, :, :, None] * values[:, query_slot_index, :, None, :]
        )
        decoding_results.append(
            jnp.einsum(
                "ghl,ghlm->ghm",
                acceptance_gate_entries[:, query_slot_index],
                present_outer_product + reward_grouped[:, :, None] * address_content_product,
                precision=lax.Precision.HIGHEST,
            )
        )
        valid_rows = (query_slot_index < occupied_slot_totals)[:, None, None, None]
        present_outer_product = jnp.where(
            valid_rows,
            decay_rates[:, query_slot_index, :, :, None] * present_outer_product
            + address_content_product,
            present_outer_product,
        )
    mixed_heads = jnp.stack(decoding_results, axis=1)
    centered = mixed_heads - jnp.mean(mixed_heads, axis=-1, keepdims=True)
    spread = jnp.mean(centered * centered, axis=-1, keepdims=True)
    grouped_results = (
        centered * lax.rsqrt(spread + EPSILON) * divide_into_groups(grouped_layer_scaling)
    ).astype(jnp.bfloat16)
    return (grouped_results.reshape(grouped_results.shape[:2] + (-1,)), present_outer_product)


def last_live(inputs, occupied_slot_totals):
    pick_table = (
        jnp.arange(inputs.shape[1])[None, :, None] == (occupied_slot_totals - 1)[:, None, None]
    )
    return jnp.sum(jnp.where(pick_table, inputs, jnp.zeros_like(inputs)), axis=1)


def on_device(
    arriving_hiddens,
    occupied_slot_totals,
    former_indices,
    reconstruct_marks,
    retained_hiddens,
    carried_memory_matrices,
    lagged_previous_entries,
    pre_attention_scaling,
    pre_feedforward_scaling,
    lag_blend_fractions,
    acceptance_projection,
    address_projection,
    content_projection,
    fading_lowrank_left,
    fading_lowrank_right,
    fading_baseline_entries,
    present_item_reward,
    grouped_layer_scaling,
    attention_exit_projection,
    feedforward_address_proj,
    feedforward_content_proj,
):
    req_rows = arriving_hiddens.shape[0]
    local_heads = carried_memory_matrices.shape[1]
    model_width = pre_attention_scaling.shape[0]
    grp_index = lax.axis_index("grp")
    groups = lax.axis_size("grp")
    head_index = lax.axis_index("head")
    feature_part = model_width // lax.axis_size("head")
    offset = (former_indices // req_rows - grp_index) % groups
    source_row = former_indices % req_rows
    state_size = local_heads * ATTENTION_WIDTH * ATTENTION_WIDTH
    packed = jnp.concatenate(
        [
            carried_memory_matrices.reshape(req_rows, -1),
            lagged_previous_entries.reshape(req_rows, -1),
        ],
        axis=1,
    )
    ready_rows = jnp.take(packed, source_row, axis=0)
    moved_rows = ready_rows
    for bit_index in range((groups - 1).bit_length()):
        shifted = shifted_2(moved_rows, "grp", -(1 << bit_index))
        moved_rows = jnp.where((offset >> bit_index & 1 == 1)[:, None], shifted, moved_rows)
    present_outer_product = moved_rows[:, :state_size].reshape(
        req_rows, local_heads, ATTENTION_WIDTH, ATTENTION_WIDTH
    )
    shift_part = moved_rows[:, state_size:].reshape(req_rows, 2, feature_part)
    mark_rank = jnp.cumsum(reconstruct_marks) - reconstruct_marks
    slot_table = (
        (reconstruct_marks[None, :] == 1) & (mark_rank[None, :] == jnp.arange(REB)[:, None])
    ).astype(jnp.bfloat16)
    chosen = jnp.einsum(
        "sn,ntd->std", slot_table, retained_hiddens, preferred_element_type=jnp.float32
    ).astype(jnp.bfloat16)
    full_tokens, full_chosen = (
        lax.all_gather(arriving_hiddens, "head", axis=2, tiled=True),
        lax.all_gather(chosen, "head", axis=2, tiled=True),
    )
    full_shift = lax.all_gather(shift_part.astype(jnp.bfloat16), "head", axis=2, tiled=True).astype(
        shift_part.dtype
    )
    rebuilt, last_hist = rebuild(
        full_chosen,
        pre_attention_scaling,
        lag_blend_fractions,
        address_projection,
        content_projection,
        fading_lowrank_left,
        fading_lowrank_right,
        fading_baseline_entries,
    )
    pick_slot = jnp.clip(mark_rank, 0, REB - 1)
    marked = reconstruct_marks == 1
    present_outer_product = jnp.where(
        marked[:, None, None, None], jnp.take(rebuilt, pick_slot, axis=0), present_outer_product
    )
    lagged_entry = jnp.where(
        marked[:, None], jnp.take(last_hist, pick_slot, axis=0), full_shift[:, 0]
    )
    standardized_entry = layer_norm(full_tokens.astype(jnp.float32), pre_attention_scaling)
    grouped_results, present_outer_product = attention_result(
        standardized_entry,
        lagged_entry,
        present_outer_product,
        occupied_slot_totals,
        lag_blend_fractions,
        acceptance_projection,
        address_projection,
        content_projection,
        fading_lowrank_left,
        fading_lowrank_right,
        fading_baseline_entries,
        present_item_reward,
        grouped_layer_scaling,
    )
    flat_heads = grouped_results.reshape(-1, grouped_results.shape[-1])
    mix_total = lax.psum(
        jnp.dot(flat_heads, attention_exit_projection, preferred_element_type=jnp.float32).astype(
            jnp.bfloat16
        ),
        "head",
    ).astype(jnp.float32)
    middle = (full_tokens.astype(jnp.float32) + mix_total.reshape(full_tokens.shape)).astype(
        jnp.bfloat16
    )
    middle_local = lax.dynamic_slice_in_dim(middle, head_index * feature_part, feature_part, 2)
    second = layer_norm(middle.astype(jnp.float32), pre_feedforward_scaling)
    current = second.astype(jnp.float32)
    previous = jnp.concatenate([full_shift[:, 1][:, None], current[:, :-1]], axis=1)
    hidden = jnp.square(
        jax.nn.relu(
            project(blend_rows(current, previous, lag_blend_fractions[4]), feedforward_address_proj)
        )
    ).astype(jnp.bfloat16)
    flat_hidden = hidden.reshape(-1, hidden.shape[-1])
    ffn_rows = lax.psum_scatter(
        lax.dot_general(
            feedforward_content_proj,
            flat_hidden,
            (((0,), (1,)), ((), ())),
            preferred_element_type=jnp.float32,
        ).astype(jnp.bfloat16),
        "head",
        scatter_dimension=0,
        tiled=True,
    ).astype(jnp.float32)
    result = (middle_local.astype(jnp.float32) + ffn_rows.T.reshape(middle_local.shape)).astype(
        jnp.bfloat16
    )
    valid_rows = jnp.arange(arriving_hiddens.shape[1])[None, :] < occupied_slot_totals[:, None]
    result = jnp.where(valid_rows[..., None], result, jnp.zeros_like(result))
    time_last = lax.dynamic_slice_in_dim(
        last_live(standardized_entry.astype(jnp.float32), occupied_slot_totals),
        head_index * feature_part,
        feature_part,
        1,
    )
    channel_last = lax.dynamic_slice_in_dim(
        last_live(current, occupied_slot_totals), head_index * feature_part, feature_part, 1
    )
    return (result, present_outer_product, jnp.stack([time_last, channel_last], axis=1))


def solution(mesh):
    placed = (
        P("grp", None, "head"),
        P("grp"),
        P("grp"),
        P("grp"),
        P("grp", None, "head"),
        P("grp", "head", None, None),
        P("grp", None, "head"),
        P(),
        P(),
        P(),
        P(None, "head"),
        P(None, "head"),
        P(None, "head"),
        P(),
        P(None, "head"),
        P("head"),
        P("head"),
        P("head"),
        P("head", None),
        P(None, "head"),
        P("head", None),
    )
    return jax.shard_map(
        on_device,
        mesh=mesh,
        in_specs=placed,
        out_specs=(P("grp", None, "head"), P("grp", "head", None, None), P("grp", None, "head")),
        check_vma=False,
    )
```

profile of v0, /device:TPU:8, one launch (start us, length us, event | category | flops | bytes accessed | tf_op | source)
XLA Modules:
  0.0 305.9 jit_solution(17810951148594460560)
XLA Ops:
  7.2 1.4 and_compare_fusion.5
  9.4 1.6 reshape.289
  11.8 0.9 broadcast_select_fusion
  15.0 12.6 %all_gather.10 = bf16[2,32,2048]{2,1,0:T(8,128)(2,1)S(1)} all-gather(bf16[2,32,512]{2,1,0:T(8,128)(2,1)S(1)} %copy.145), channel_id=1, replica_groups=mesh['grp'=64,'head'=4] {'head'}, dimensions={2}, use_global_device_ids=true | all-gather | bytes 327680 | tf_op jit(solution)/shard_map/all_gather | solution.py:230
  28.1 0.9 copy-done.6
  29.0 1.2 broadcast_select_fusion.1
  30.2 8.3 %collective-permute-start.1 = (f32[8,17408]{1,0:T(8,128)S(1)}, f32[8,17408]{1,0:T(8,128)}, u32[]{:S(2)}, u32[]{:S(2)}) collective-permute-start(f32[8,17408]{1,0:T(8,128)S(1)} %broadcast_select_fusion.1), channel_id=1, source_target_pairs={{0,248},{4,252},{8,0},{12,4},{16,8},{20,12},{24,16},{28,20},{32,24... | collective-permute-start | bytes 1671176 | tf_op jit(solution)/shard_map/ppermute | solution.py:14
  38.5 1.4 fusion.15
  40.1 2.3 copy.80
  42.4 1.5 copy.81
  43.9 2.4 convolution_bitcast_fusion.1
  46.3 2.4 convolution_bitcast_fusion
  48.7 1.4 broadcast_select_fusion.2
  50.0 5.3 %collective-permute-start.2 = (f32[8,17408]{1,0:T(8,128)S(1)}, f32[8,17408]{1,0:T(8,128)}, u32[]{:S(2)}, u32[]{:S(2)}) collective-permute-start(f32[8,17408]{1,0:T(8,128)S(1)} %broadcast_select_fusion.2), channel_id=1, source_target_pairs={{0,240},{4,244},{8,248},{12,252},{16,0},{20,4},{24,8},{28,12},{32,... | collective-permute-start | bytes 1671176 | tf_op jit(solution)/shard_map/ppermute | solution.py:14
  55.4 34.7 %while.11 = (s32[]{:T(128)}, f32[2,4,64,64]{3,2,1,0:T(8,128)S(1)}, f32[32,2,4,64]{3,2,1,0:T(4,128)S(1)}, f32[32,2,4,64]{3,0,2,1:T(8,128)S(1)}, f32[32,2,4,64]{3,0,2,1:T(8,128)}, /*index=5*/s32[]{:T(128)}, s32[]{:T(128)}) while((s32[]{:T(128)}, f32[2,4,64,64]{3,2,1,0:T(8,128)S(1)}, f32[32,2,4,64]{3,2,1,0:T(4,128)S(1)}, ...), condition=%wide.region_6.7_spmd.clone, body=%wide.region_5.6_spmd.clone.sunk | while | flops 131075 | bytes 280679 | solution.py:97
  56.4 0.8 constant_dynamic-slice_fusion.3
  57.5 0.8 constant_dynamic-slice_fusion.3
  63.0 0.8 constant_dynamic-slice_fusion.3
  68.4 0.8 constant_dynamic-slice_fusion.3
  78.2 0.8 constant_dynamic-slice_fusion.3
  83.6 0.8 constant_dynamic-slice_fusion.3
  89.0 0.8 constant_dynamic-slice_fusion.3
  90.1 0.9 slice.126
  91.0 1.4 mul.345
  92.4 2.3 copy.77
  94.7 12.0 %all_gather.9 = bf16[8,4,2048]{2,1,0:T(4,128)(2,1)S(1)} all-gather(bf16[8,4,512]{2,1,0:T(4,128)(2,1)S(1)} %copy-done.16), channel_id=1, replica_groups=mesh['grp'=64,'head'=4] {'head'}, dimensions={2}, use_global_device_ids=true | all-gather | bytes 163840 | tf_op jit(solution)/shard_map/all_gather | solution.py:229
  106.7 1.2 broadcast_select_fusion.3
  108.7 18.3 %collective-permute-done.3 = f32[8,17408]{1,0:T(8,128)S(1)} collective-permute-done((f32[8,17408]{1,0:T(8,128)S(1)}, f32[8,17408]{1,0:T(8,128)S(1)}, u32[]{:S(2)}, u32[]{:S(2)}) %collective-permute-start.3) | collective-permute-done | bytes 557088 | tf_op jit(solution)/shard_map/ppermute | solution.py:14
  128.1 38.4 %collective-permute-done.4 = f32[8,17408]{1,0:T(8,128)S(1)} collective-permute-done((f32[8,17408]{1,0:T(8,128)S(1)}, f32[8,17408]{1,0:T(8,128)S(1)}, u32[]{:S(2)}, u32[]{:S(2)}) %collective-permute-start.4) | collective-permute-done | bytes 557088 | tf_op jit(solution)/shard_map/ppermute | solution.py:14
  168.1 18.2 %collective-permute-done.5 = f32[8,17408]{1,0:T(8,128)} collective-permute-done((f32[8,17408]{1,0:T(8,128)S(1)}, f32[8,17408]{1,0:T(8,128)}, u32[]{:S(2)}, u32[]{:S(2)}) %collective-permute-start.5) | collective-permute-done | bytes 557088 | tf_op jit(solution)/shard_map/ppermute | solution.py:14
  186.3 1.2 broadcast_select_fusion.6
  187.5 0.8 slice.132
  188.4 12.0 %all_gather.11 = bf16[8,2,2048]{2,0,1:T(8,128)(2,1)S(1)} all-gather(bf16[8,2,512]{2,0,1:T(8,128)(2,1)S(1)} %bitcast.193), channel_id=1, replica_groups=mesh['grp'=64,'head'=4] {'head'}, dimensions={2}, use_global_device_ids=true | all-gather | bytes 81920 | tf_op jit(solution)/shard_map/all_gather | solution.py:232
  202.5 1.1 fusion.99
  203.6 1.5 reshape.292
  205.2 1.9 fusion.105
  207.1 1.9 fusion.103
  209.1 1.8 fusion.101
  211.0 4.1 %fusion.36 = (f32[8,4,64,64]{3,2,1,0:T(8,128)}, f32[8,4,64,64]{3,2,1,0:T(8,128)S(1)}) fusion(f32[8,4,64]{2,1,0:T(4,128)S(1)} %copy-done.13, f32[8,4,64]{2,1,0:T(4,128)S(1)} %copy.94, f32[8,4,64]{2,1,0:T(4,128)S(1)} %copy.93, f32[8,4,64]{2,1,0:T(4,128)S(1)} %copy-done.12, f32[8,4,64]{2,1,0:T(4,128)S(1)} %copy.92, f32[8,4,64]{2,1,0:T(4,128)S(1)} %copy.91, ...), kind=kLoop, calls=%fused_computation.49 | loop fusion | flops 2359296 | bytes 2195504 | tf_op jit(solution)/shard_map/jit(_where)/select_n | solution.py:150
  215.2 2.8 fusion.34
  218.0 2.3 fusion.30
  220.3 1.7 fusion.26
  222.0 1.2 fusion.22
  225.3 40.4 %all-reduce.3.cloned.1.call-done = bf16[8,4,2048]{2,1,0:T(4,128)(2,1)} async-done(((bf16[8,4,2048]{2,1,0:T(4,128)(2,1)}), bf16[8,4,2048]{2,1,0:T(4,128)(2,1)}) %all-reduce.3.cloned.1.call-update) | async-done | bytes 131088 | tf_op jit(solution)/shard_map/psum | solution.py:270
  265.7 1.1 convert_reduce_fusion.2
  267.8 2.7 fusion.10
  270.6 3.4 %fusion.3 = bf16[2048,32]{0,1:T(8,128)(2,1)} fusion(bf16[32,896]{1,0:T(8,128)(2,1)S(1)} %reshape.296, bf16[896,2048]{1,0:T(8,128)(2,1)} %param.43), kind=kOutput, calls=%fused_computation.12 | convolution fusion | flops 117506048 | bytes 3858432 | tf_op jit(solution)/shard_map/dot_general | solution.py:290
  274.7 22.9 %reduce-scatter.2.cloned.1.call-done = bf16[512,32]{0,1:T(8,128)(2,1)} async-done(((bf16[2048,32]{0,1:T(8,128)(2,1)}), bf16[512,32]{0,1:T(8,128)(2,1)}) %reduce-scatter.2.cloned.1.call-update) | async-done | bytes 32784 | tf_op jit(solution)/shard_map/reduce_scatter | solution.py:289
  (250 shorter events, 43.8 us)
Async XLA Ops:
  7.2 216.6 %copy-start = (bf16[256,2048]{1,0:T(8,128)(2,1)S(1)}, bf16[256,2048]{1,0:T(8,128)(2,1)}, u32[]{:S(2)}) copy-start(bf16[256,2048]{1,0:T(8,128)(2,1)} %param.41) | copy-start | bytes 3145732
  7.2 258.5 %all-reduce.3.cloned.1.call-start = ((), (), s32[]{:S(2)}) async-start(), calls=%async_computation.1 | async-start | bytes 262144 | tf_op jit(solution)/shard_map/psum | solution.py:270
  10.9 1.8 copy-start.34
  10.9 3.1 %copy-start.18 = (f32[5,2048]{1,0:T(8,128)S(1)}, f32[5,2048]{1,0:T(8,128)}, u32[]{:S(2)}) copy-start(f32[5,2048]{1,0:T(8,128)} %param.32) | copy-start | bytes 122884
  11.0 3.7 %copy-start.8 = (bf16[8,32,512]{2,1,0:T(8,128)(2,1)S(1)}, bf16[8,32,512]{2,1,0:T(8,128)(2,1)}, u32[]{:S(2)}) copy-start(bf16[8,32,512]{2,1,0:T(8,128)(2,1)} %param.27) | copy-start | bytes 786436
  11.0 16.9 %copy-start.9 = (f32[2048]{0:T(1024)S(1)}, f32[2048]{0:T(1024)}, u32[]{:S(2)}) copy-start(f32[2048]{0:T(1024)} %param.30) | copy-start | bytes 24580
  11.8 26.7 %copy-start.17 = (bf16[64,256]{1,0:T(8,128)(2,1)S(1)}, bf16[64,256]{1,0:T(8,128)(2,1)}, u32[]{:S(2)}) copy-start(bf16[64,256]{1,0:T(8,128)(2,1)} %param.37) | copy-start | bytes 98308
  11.8 26.7 %copy-start.30 = (f32[256]{0:T(256)S(1)}, f32[256]{0:T(256)}, u32[]{:S(2)}) copy-start(f32[256]{0:T(256)} %param.38) | copy-start | bytes 3076
  12.7 15.4 %collective-permute-start = (f32[8,17408]{1,0:T(8,128)}, f32[8,17408]{1,0:T(8,128)S(1)}, u32[]{:S(2)}, u32[]{:S(2)}) collective-permute-start(f32[8,17408]{1,0:T(8,128)} %broadcast_select_fusion), channel_id=1, source_target_pairs={{0,252},{4,0},{8,4},{12,8},{16,12},{20,16},{24,20},{28,24},{32,28}... | collective-permute-start | bytes 1671176 | tf_op jit(solution)/shard_map/ppermute | solution.py:14
  13.5 187.6 %copy-start.19 = (pred[8]{0:T(512)(128)(4,1)}, pred[8]{0:T(512)(128)(4,1)S(1)}, u32[]{:S(2)}) copy-start(pred[8]{0:T(512)(128)(4,1)S(1)} %get-tuple-element.124) | copy-start | bytes 28
  14.7 25.4 %copy-start.21 = (f32[1,2048]{1,0:T(1,128)}, f32[1,2048]{1,0:T(1,128)S(1)}, u32[]{:S(2)}) copy-start(f32[1,2048]{1,0:T(1,128)S(1)} %get-tuple-element.101) | copy-start | bytes 24580
  28.1 12.0 %copy-start.5 = (f32[2,32,2048]{2,1,0:T(8,128)}, f32[2,32,2048]{2,1,0:T(8,128)S(1)}, u32[]{:S(2)}) copy-start(f32[2,32,2048]{2,1,0:T(8,128)S(1)} %fusion.133) | copy-start | bytes 1572868
  28.1 0.9 copy-start.6
  30.2 16.1 %copy-start.2 = (f32[8,17408]{1,0:T(8,128)}, f32[8,17408]{1,0:T(8,128)S(1)}, u32[]{:S(2)}) copy-start(f32[8,17408]{1,0:T(8,128)S(1)} %broadcast_select_fusion.1) | copy-start | bytes 1671172
  30.2 18.5 %collective-permute-start.1 = (f32[8,17408]{1,0:T(8,128)S(1)}, f32[8,17408]{1,0:T(8,128)}, u32[]{:S(2)}, u32[]{:S(2)}) collective-permute-start(f32[8,17408]{1,0:T(8,128)S(1)} %broadcast_select_fusion.1), channel_id=1, source_target_pairs={{0,248},{4,252},{8,0},{12,4},{16,8},{20,12},{24,16},{28,20},{32,24... | collective-permute-start | bytes 1671176 | tf_op jit(solution)/shard_map/ppermute | solution.py:14
  43.9 11.5 %copy-start.1 = (bf16[2048,256]{0,1:T(8,128)(2,1)}, bf16[2048,256]{0,1:T(8,128)(2,1)S(1)}, u32[]{:S(2)}) copy-start(bf16[2048,256]{0,1:T(8,128)(2,1)S(1)} %copy.81) | copy-start | bytes 3145732
  48.7 46.0 %copy-start.16 = (bf16[8,4,512]{2,1,0:T(4,128)(2,1)S(1)}, bf16[8,4,512]{2,1,0:T(4,128)(2,1)}, u32[]{:S(2)}) copy-start(bf16[8,4,512]{2,1,0:T(4,128)(2,1)} %param.23) | copy-start | bytes 98308
  50.0 58.1 %copy-start.35 = (s32[8]{0:T(128)S(1)}, s32[8]{0:T(128)}, u32[]{:S(2)}) copy-start(s32[8]{0:T(128)} %param.24) | copy-start | bytes 100
  50.0 56.6 %collective-permute-start.2 = (f32[8,17408]{1,0:T(8,128)S(1)}, f32[8,17408]{1,0:T(8,128)}, u32[]{:S(2)}, u32[]{:S(2)}) collective-permute-start(f32[8,17408]{1,0:T(8,128)S(1)} %broadcast_select_fusion.2), channel_id=1, source_target_pairs={{0,240},{4,244},{8,248},{12,252},{16,0},{20,4},{24,8},{28,12},{32,... | collective-permute-start | bytes 1671176 | tf_op jit(solution)/shard_map/ppermute | solution.py:14
  90.1 76.4 %copy-start.24 = (pred[8]{0:T(512)(128)(4,1)S(1)}, pred[8]{0:T(512)(128)(4,1)}, u32[]{:S(2)}) copy-start(pred[8]{0:T(512)(128)(4,1)} %get-tuple-element.125) | copy-start | bytes 28
  92.4 74.3 %copy-start.29 = (s32[8]{0:T(128)S(1)}, s32[8]{0:T(128)}, u32[]{:S(2)}) copy-start(s32[8]{0:T(128)} %get-tuple-element.87) | copy-start | bytes 100
  107.9 78.5 %copy-start.28 = (pred[8]{0:T(512)(128)(4,1)S(1)}, pred[8]{0:T(512)(128)(4,1)}, u32[]{:S(2)}) copy-start(pred[8]{0:T(512)(128)(4,1)} %get-tuple-element.89) | copy-start | bytes 28
  107.9 19.1 %collective-permute-start.3 = (f32[8,17408]{1,0:T(8,128)S(1)}, f32[8,17408]{1,0:T(8,128)S(1)}, u32[]{:S(2)}, u32[]{:S(2)}) collective-permute-start(f32[8,17408]{1,0:T(8,128)S(1)} %broadcast_select_fusion.3), channel_id=1, source_target_pairs={{0,224},{4,228},{8,232},{12,236},{16,240},{20,244},{24,248},{28,25... | collective-permute-start | bytes 1671176 | tf_op jit(solution)/shard_map/ppermute | solution.py:14
  127.1 39.4 %collective-permute-start.4 = (f32[8,17408]{1,0:T(8,128)S(1)}, f32[8,17408]{1,0:T(8,128)S(1)}, u32[]{:S(2)}, u32[]{:S(2)}) collective-permute-start(f32[8,17408]{1,0:T(8,128)S(1)} %broadcast_select_fusion.4), channel_id=1, source_target_pairs={{0,192},{4,196},{8,200},{12,204},{16,208},{20,212},{24,216},{28,22... | collective-permute-start | bytes 1671176 | tf_op jit(solution)/shard_map/ppermute | solution.py:14
  166.5 34.6 %copy-start.23 = (pred[8]{0:T(512)(128)(4,1)S(1)}, pred[8]{0:T(512)(128)(4,1)}, u32[]{:S(2)}) copy-start(pred[8]{0:T(512)(128)(4,1)} %get-tuple-element.86) | copy-start | bytes 28
  166.5 34.7 %copy-start.22 = (f32[1,2048]{1,0:T(1,128)S(1)}, f32[1,2048]{1,0:T(1,128)}, u32[]{:S(2)}) copy-start(f32[1,2048]{1,0:T(1,128)} %copy-done.21) | copy-start | bytes 24580
  166.5 34.7 %copy-start.36 = (bf16[2048,64]{0,1:T(8,128)(2,1)S(1)}, bf16[2048,64]{0,1:T(8,128)(2,1)}, u32[]{:S(2)}) copy-start(bf16[2048,64]{0,1:T(8,128)(2,1)} %param.36) | copy-start | bytes 786436
  166.6 19.7 %collective-permute-start.5 = (f32[8,17408]{1,0:T(8,128)S(1)}, f32[8,17408]{1,0:T(8,128)}, u32[]{:S(2)}, u32[]{:S(2)}) collective-permute-start(f32[8,17408]{1,0:T(8,128)S(1)} %broadcast_select_fusion.5), channel_id=1, source_target_pairs={{0,128},{4,132},{8,136},{12,140},{16,144},{20,148},{24,152},{28,15... | collective-permute-start | bytes 1671176 | tf_op jit(solution)/shard_map/ppermute | solution.py:14
  167.3 34.4 %copy-start.31 = (f32[256]{0:T(256)S(1)}, f32[256]{0:T(256)}, u32[]{:S(2)}) copy-start(f32[256]{0:T(256)} %param.38) | copy-start | bytes 3076
  200.4 0.6 copy-start.3
  203.6 5.5 %copy-start.7 = (bf16[8,4,2048,1]{2,1,0,3:T(4,128)(2,1)S(1)}, bf16[8,4,2048,1]{2,1,0,3:T(4,128)(2,1)}, u32[]{:S(2)}) copy-start(bf16[8,4,2048,1]{2,1,0,3:T(4,128)(2,1)} %get-tuple-element.97) | copy-start | bytes 393220
  205.1 5.9 %copy-start.10 = (f32[8,4,64]{2,1,0:T(4,128)S(1)}, f32[8,4,64]{2,1,0:T(4,128)}, u32[]{:S(2)}) copy-start(f32[8,4,64]{2,1,0:T(4,128)} %get-tuple-element.111) | copy-start | bytes 24580
  205.1 5.9 %copy-start.11 = (f32[8,4,64]{2,1,0:T(4,128)S(1)}, f32[8,4,64]{2,1,0:T(4,128)}, u32[]{:S(2)}) copy-start(f32[8,4,64]{2,1,0:T(4,128)} %get-tuple-element.108) | copy-start | bytes 24580
  205.2 5.9 %copy-start.12 = (f32[8,4,64]{2,1,0:T(4,128)S(1)}, f32[8,4,64]{2,1,0:T(4,128)}, u32[]{:S(2)}) copy-start(f32[8,4,64]{2,1,0:T(4,128)} %get-tuple-element.110) | copy-start | bytes 24580
  205.2 5.9 %copy-start.13 = (f32[8,4,64]{2,1,0:T(4,128)S(1)}, f32[8,4,64]{2,1,0:T(4,128)}, u32[]{:S(2)}) copy-start(f32[8,4,64]{2,1,0:T(4,128)} %get-tuple-element.109) | copy-start | bytes 24580
  207.1 8.0 %copy-start.20 = (f32[4,64]{1,0:T(4,128)S(1)}, f32[4,64]{1,0:T(4,128)}, u32[]{:S(2)}) copy-start(f32[4,64]{1,0:T(4,128)} %mul.345) | copy-start | bytes 3076
  207.1 8.0 %copy-start.25 = (pred[8]{0:T(512)(128)(4,1)S(1)}, pred[8]{0:T(512)(128)(4,1)}, u32[]{:S(2)}) copy-start(pred[8]{0:T(512)(128)(4,1)} %get-tuple-element.133) | copy-start | bytes 28
  207.1 8.0 %copy-start.26 = (pred[8]{0:T(512)(128)(4,1)S(1)}, pred[8]{0:T(512)(128)(4,1)}, u32[]{:S(2)}) copy-start(pred[8]{0:T(512)(128)(4,1)} %get-tuple-element.135) | copy-start | bytes 28
  207.1 8.0 %copy-start.27 = (pred[8]{0:T(512)(128)(4,1)S(1)}, pred[8]{0:T(512)(128)(4,1)}, u32[]{:S(2)}) copy-start(pred[8]{0:T(512)(128)(4,1)} %get-tuple-element.134) | copy-start | bytes 28
  218.0 5.8 %copy-start.33 = (f32[256]{0:T(256)S(1)}, f32[256]{0:T(256)}, u32[]{:S(2)}) copy-start(f32[256]{0:T(256)} %param.40) | copy-start | bytes 3076
  220.3 4.9 %copy-start.37 = (s32[8]{0:T(128)S(1)}, s32[8]{0:T(128)}, u32[]{:S(2)}) copy-start(s32[8]{0:T(128)} %broadcast_add_fusion) | copy-start | bytes 100
  220.3 4.9 %copy-start.4 = (bf16[8,2,2048]{2,0,1:T(8,128)(2,1)S(1)}, bf16[8,2,2048]{2,0,1:T(8,128)(2,1)}, u32[]{:S(2)}) copy-start(bf16[8,2,2048]{2,0,1:T(8,128)(2,1)} %copy-done.3) | copy-start | bytes 196612
  220.3 46.7 %copy-start.14 = (f32[2048]{0:T(1024)S(1)}, f32[2048]{0:T(1024)}, u32[]{:S(2)}) copy-start(f32[2048]{0:T(1024)} %param.31) | copy-start | bytes 24580
  220.3 46.9 %copy-start.15 = (f32[1,2048]{1,0:T(1,128)S(1)}, f32[1,2048]{1,0:T(1,128)}, u32[]{:S(2)}) copy-start(f32[1,2048]{1,0:T(1,128)} %get-tuple-element.99) | copy-start | bytes 24580
  224.8 72.8 %reduce-scatter.2.cloned.1.call-start = ((), (), s32[]{:S(2)}) async-start(), calls=%async_computation.2 | async-start | bytes 163840 | tf_op jit(solution)/shard_map/reduce_scatter | solution.py:289
  270.5 27.9 %copy-start.32 = (pred[8,4]{1,0:T(8,128)(4,1)S(1)}, pred[8,4]{1,0:T(8,128)(4,1)}, u32[]{:S(2)}) copy-start(pred[8,4]{1,0:T(8,128)(4,1)} %iota_compare_fusion.1) | copy-start | bytes 100
Sparse Core Ops, SparseCore 0:
  225.0 40.6 all-reduce.2
  274.2 23.3 reduce-scatter.1
where the time goes:
time: 309 us; the launch traced here: 306 us
  waiting for transfers between devices  138 us (45%)
  local copies, waits for them, and re-layouts  44.9 us (15%)
  blocking collectives  36.6 us (12%)
  other arithmetic  29.1 us (9%)
  matrix products  27 us (9%)
  between operations  14.9 us (5%)
  starting transfers between devices  14.1 us (5%)
    ppermute x6, waiting for transfers between devices, shifted_2(): return lax.ppermute(value, axis, pairs)  74.9 us
    psum x1, waiting for transfers between devices, on_device(): lax.psum(jnp.dot(flat_heads, attention_exit_projection, preferred_element...  40.4 us
    dynamic_slice x32, local copies, waits for them, and re-layouts, rebuild(): lax.scan(advance, start_state, (jnp.moveaxis(key_rows, 1, 0), jnp.moveaxi...  24.8 us
    reduce_scatter x1, waiting for transfers between devices, on_device(): lax.psum_scatter(lax.dot_general(feedforward_content_proj, flat_hidden, (...  22.9 us
    dot_general x9, matrix products, project(): result = jnp.dot(flat_rows, weight, preferred_element_type=jnp.float32)  15.1 us
    ppermute x6, starting transfers between devices, shifted_2(): return lax.ppermute(value, axis, pairs)  13.8 us
    all_gather x1, blocking collectives, on_device(): lax.all_gather(chosen, 'head', axis=2, tiled=True)  12.6 us
    all_gather x1, blocking collectives, on_device(): lax.all_gather(shift_part.astype(jnp.bfloat16), 'head', axis=2, tiled=True)  12 us
  transfers between devices with their start and end apart: 8, of which 5 were waited for; matrix products, arithmetic and copies ran while one was open for 18% of the time, Pallas kernels for 0%

commit v1 on v0

--- a/solution.py
+++ b/solution.py
@@ -6,6 +6,19 @@
 ATTENTION_WIDTH = 64
 REB = 2
 EPSILON = 1e-05
+
+
+def gather_around(x, axis, dim):
+    ways = lax.axis_size(axis)
+    up = [(d, (d + 1) % ways) for d in range(ways)]
+    down = [(d, (d - 1) % ways) for d in range(ways)]
+    earlier, later = ([x], [x])
+    for _ in range(ways // 2):
+        earlier.append(lax.ppermute(earlier[-1], axis, up))
+    for _ in range((ways - 1) // 2):
+        later.append(lax.ppermute(later[-1], axis, down))
+    line = jnp.concatenate([*earlier[::-1], *later[1:]], axis=dim)
+    return jnp.roll(line, (lax.axis_index(axis) - ways // 2) * x.shape[dim], axis=dim)
 
 
 def shifted_2(value, axis, steps):
@@ -227,7 +240,7 @@
     ).astype(jnp.bfloat16)
     full_tokens, full_chosen = (
         lax.all_gather(arriving_hiddens, "head", axis=2, tiled=True),
-        lax.all_gather(chosen, "head", axis=2, tiled=True),
+        gather_around(chosen, "head", 2),
     )
     full_shift = lax.all_gather(shift_part.astype(jnp.bfloat16), "head", axis=2, tiled=True).astype(
         shift_part.dtype

time: 309 us -> 333 us (1.078)
  local copies, waits for them, and re-layouts: 44.9 us -> 65 us
  blocking collectives: 36.6 us -> 28.8 us
  waiting for transfers between devices: 138 us -> 145 us
    mul x32, local copies, waits for them, and re-layouts: 0.23 us -> 21.9 us  [advance(): decay_step[..., :, None] * present_outer_product]
    all_gather x1 -> x0, blocking collectives: 12.6 us -> none  [on_device(): lax.all_gather(chosen, 'head', axis=2, tiled=True)]
    psum x1, waiting for transfers between devices: 40.4 us -> 50.1 us  [on_device(): lax.psum(jnp.dot(flat_heads, attention_exit_projection, preferred_element...]
    ppermute x6, waiting for transfers between devices: 74.9 us -> 68.8 us  [shifted_2(): return lax.ppermute(value, axis, pairs)]
    ppermute x6, starting transfers between devices: 13.8 us -> 8.33 us  [shifted_2(): return lax.ppermute(value, axis, pairs)]
    ppermute x0 -> x3, starting transfers between devices: none -> 4.85 us  [the longest x1 2.76 us: gather_around(): later.append(lax.ppermute(later[-1], axis, down))]
    all_gather x1, blocking collectives: 12 us -> 16.8 us  [on_device(): lax.all_gather(shift_part.astype(jnp.bfloat16), 'head', axis=2, tiled=True)]
    unnamed x82 -> x81, local copies, waits for them, and re-layouts: 9.13 us -> 6.83 us
  transfers between devices with their start and end apart: 8 -> 11, of which waited for: 5 -> 7; matrix products, arithmetic and copies ran while one was open for 18% -> 25% of each run, Pallas kernels for 0% -> 0%
where the time goes in v1:
time: 333 us; the launch traced here: 329 us
  waiting for transfers between devices  145 us (44%)
  local copies, waits for them, and re-layouts  65 us (20%)
  other arithmetic  31.4 us (9%)
  matrix products  29.6 us (9%)
  blocking collectives  28.8 us (9%)
  between operations  14.9 us (4%)
  starting transfers between devices  13.5 us (4%)
    ppermute x6, waiting for transfers between devices, shifted_2(): return lax.ppermute(value, axis, pairs)  68.8 us
    psum x1, waiting for transfers between devices, on_device(): lax.psum(jnp.dot(flat_heads, attention_exit_projection, preferred_element...  50.1 us
    dynamic_slice x32, local copies, waits for them, and re-layouts, rebuild(): lax.scan(advance, start_state, (jnp.moveaxis(key_rows, 1, 0), jnp.moveaxi...  25 us
    reduce_scatter x1, waiting for transfers between devices, on_device(): lax.psum_scatter(lax.dot_general(feedforward_content_proj, flat_hidden, (...  22.9 us
    mul x32, local copies, waits for them, and re-layouts, advance(): decay_step[..., :, None] * present_outer_product  21.9 us
    all_gather x1, blocking collectives, on_device(): lax.all_gather(shift_part.astype(jnp.bfloat16), 'head', axis=2, tiled=True)  16.8 us
    dot_general x9, matrix products, project(): result = jnp.dot(flat_rows, weight, preferred_element_type=jnp.float32)  16.7 us
    all_gather x1, blocking collectives, on_device(): lax.all_gather(arriving_hiddens, 'head', axis=2, tiled=True)  12 us
  transfers between devices with their start and end apart: 11, of which 7 were waited for; matrix products, arithmetic and copies ran while one was open for 25% of the time, Pallas kernels for 0%

profile of v1, /device:TPU:8, one launch (start us, length us, event | category | flops | bytes accessed | tf_op | source)
XLA Modules:
  0.0 328.6 jit_solution(14530247216234283973)
XLA Ops:
  7.2 0.9 reduce-window.9
  8.1 1.3 compare_and_fusion.1
  9.4 1.2 fusion.90
  11.2 2.8 collective-permute-start.2
  14.0 1.3 and_compare_fusion.5
  16.0 1.6 reshape.289
  18.5 0.9 broadcast_select_fusion
  21.3 12.0 %all_gather.6 = bf16[8,4,2048]{2,1,0:T(4,128)(2,1)S(1)} all-gather(bf16[8,4,512]{2,1,0:T(4,128)(2,1)S(1)} %copy-done.11), channel_id=1, replica_groups=mesh['grp'=64,'head'=4] {'head'}, dimensions={2}, use_global_device_ids=true | all-gather | bytes 163840 | tf_op jit(solution)/shard_map/all_gather | solution.py:242
  35.1 2.3 copy.77
  37.4 1.4 copy.80
  38.8 1.5 copy.81
  40.3 2.1 collective-permute-start.1
  43.1 2.8 collective-permute-done.1
  45.9 1.2 broadcast_select_fusion.1
  47.1 8.0 %collective-permute-start.4 = (f32[8,17408]{1,0:T(8,128)S(1)}, f32[8,17408]{1,0:T(8,128)S(1)}, u32[]{:S(2)}, u32[]{:S(2)}) collective-permute-start(f32[8,17408]{1,0:T(8,128)S(1)} %broadcast_select_fusion.1), channel_id=1, source_target_pairs={{0,248},{4,252},{8,0},{12,4},{16,8},{20,12},{24,16},{28,20},{32,24... | collective-permute-start | bytes 1671176 | tf_op jit(solution)/shard_map/ppermute | solution.py:27
  55.1 18.9 %collective-permute-done.4 = f32[8,17408]{1,0:T(8,128)S(1)} collective-permute-done((f32[8,17408]{1,0:T(8,128)S(1)}, f32[8,17408]{1,0:T(8,128)S(1)}, u32[]{:S(2)}, u32[]{:S(2)}) %collective-permute-start.4) | collective-permute-done | bytes 557088 | tf_op jit(solution)/shard_map/ppermute | solution.py:27
  74.7 10.8 %collective-permute-done.5 = f32[8,17408]{1,0:T(8,128)S(1)} collective-permute-done((f32[8,17408]{1,0:T(8,128)S(1)}, f32[8,17408]{1,0:T(8,128)S(1)}, u32[]{:S(2)}, u32[]{:S(2)}) %collective-permute-start.5) | collective-permute-done | bytes 557088 | tf_op jit(solution)/shard_map/ppermute | solution.py:27
  86.4 1.0 fusion.134
  87.3 18.5 %collective-permute-done.6 = f32[8,17408]{1,0:T(8,128)S(1)} collective-permute-done((f32[8,17408]{1,0:T(8,128)S(1)}, f32[8,17408]{1,0:T(8,128)S(1)}, u32[]{:S(2)}, u32[]{:S(2)}) %collective-permute-start.6) | collective-permute-done | bytes 557088 | tf_op jit(solution)/shard_map/ppermute | solution.py:27
  106.1 1.7 fusion.15
  108.6 2.8 convolution_bitcast_fusion.1
  111.4 2.4 convolution_bitcast_fusion
  113.8 20.6 %collective-permute-done.7 = f32[8,17408]{1,0:T(8,128)} collective-permute-done((f32[8,17408]{1,0:T(8,128)S(1)}, f32[8,17408]{1,0:T(8,128)}, u32[]{:S(2)}, u32[]{:S(2)}) %collective-permute-start.7) | collective-permute-done | bytes 557088 | tf_op jit(solution)/shard_map/ppermute | solution.py:27
  134.4 1.2 broadcast_select_fusion.5
  135.7 56.4 %while.11 = (s32[]{:T(128)}, f32[2,4,64,64]{3,2,1,0:T(8,128)S(1)}, f32[32,2,4,64]{3,2,1,0:T(4,128)}, f32[32,2,4,64]{3,0,2,1:T(8,128)}, f32[32,2,4,64]{3,0,2,1:T(8,128)}, /*index=5*/s32[]{:T(128)}, s32[]{:T(128)}) while((s32[]{:T(128)}, f32[2,4,64,64]{3,2,1,0:T(8,128)S(1)}, f32[32,2,4,64]{3,2,1,0:T(4,128)}, ...), condition=%wide.region_6.7_spmd.clone, body=%wide.region_5.6_spmd.clone.sunk | while | flops 131075 | bytes 280679 | solution.py:110
  136.4 0.8 constant_dynamic-slice_fusion.3
  139.9 0.8 constant_dynamic-slice_fusion.3
  143.4 0.8 constant_dynamic-slice_fusion.3
  192.1 0.9 slice.126
  194.3 1.2 broadcast_select_fusion.6
  195.5 0.8 slice.132
  196.3 16.8 %all_gather.7 = bf16[8,2,2048]{2,0,1:T(8,128)(2,1)S(1)} all-gather(bf16[8,2,512]{2,0,1:T(8,128)(2,1)S(1)} %bitcast.193), channel_id=1, replica_groups=mesh['grp'=64,'head'=4] {'head'}, dimensions={2}, use_global_device_ids=true | all-gather | bytes 81920 | tf_op jit(solution)/shard_map/all_gather | solution.py:245
  213.3 1.4 fusion.20
  215.6 1.1 fusion.99
  216.7 1.5 reshape.292
  218.2 1.9 fusion.105
  220.1 1.9 fusion.103
  222.1 1.8 fusion.101
  224.0 4.1 %fusion.36 = (f32[8,4,64,64]{3,2,1,0:T(8,128)}, f32[8,4,64,64]{3,2,1,0:T(8,128)S(1)}) fusion(f32[8,4,64]{2,1,0:T(4,128)S(1)} %copy-done.8, f32[8,4,64]{2,1,0:T(4,128)S(1)} %copy.94, f32[8,4,64]{2,1,0:T(4,128)S(1)} %copy.93, f32[8,4,64]{2,1,0:T(4,128)S(1)} %copy-done.7, f32[8,4,64]{2,1,0:T(4,128)S(1)} %copy.92, f32[8,4,64]{2,1,0:T(4,128)S(1)} %copy.91, ...), kind=kLoop, calls=%fused_computation.49 | loop fusion | flops 2359296 | bytes 2195504 | tf_op jit(solution)/shard_map/jit(_where)/select_n | solution.py:163
  228.1 2.8 fusion.34
  231.0 2.3 fusion.30
  233.2 1.7 fusion.26
  235.0 1.2 fusion.22
  238.2 50.1 %all-reduce.3.cloned.1.call-done = bf16[8,4,2048]{2,1,0:T(4,128)(2,1)} async-done(((bf16[8,4,2048]{2,1,0:T(4,128)(2,1)}), bf16[8,4,2048]{2,1,0:T(4,128)(2,1)}) %all-reduce.3.cloned.1.call-update) | async-done | bytes 131088 | tf_op jit(solution)/shard_map/psum | solution.py:283
  288.4 1.1 convert_reduce_fusion.2
  290.5 2.7 fusion.10
  293.3 3.4 %fusion.3 = bf16[2048,32]{0,1:T(8,128)(2,1)} fusion(bf16[32,896]{1,0:T(8,128)(2,1)S(1)} %reshape.296, bf16[896,2048]{1,0:T(8,128)(2,1)} %param.43), kind=kOutput, calls=%fused_computation.12 | convolution fusion | flops 117506048 | bytes 3858432 | tf_op jit(solution)/shard_map/dot_general | solution.py:303
  297.4 22.9 %reduce-scatter.2.cloned.1.call-done = bf16[512,32]{0,1:T(8,128)(2,1)} async-done(((bf16[2048,32]{0,1:T(8,128)(2,1)}), bf16[512,32]{0,1:T(8,128)(2,1)}) %reduce-scatter.2.cloned.1.call-update) | async-done | bytes 32784 | tf_op jit(solution)/shard_map/reduce_scatter | solution.py:302
  (255 shorter events, 70.1 us)
Async XLA Ops:
  7.2 229.6 %copy-start = (bf16[256,2048]{1,0:T(8,128)(2,1)S(1)}, bf16[256,2048]{1,0:T(8,128)(2,1)}, u32[]{:S(2)}) copy-start(bf16[256,2048]{1,0:T(8,128)(2,1)} %param.41) | copy-start | bytes 3145732
  7.2 281.2 %all-reduce.3.cloned.1.call-start = ((), (), s32[]{:S(2)}) async-start(), calls=%async_computation.1 | async-start | bytes 262144 | tf_op jit(solution)/shard_map/psum | solution.py:283
  9.4 6.6 %copy-start.14 = (pred[8]{0:T(512)(128)(4,1)}, pred[8]{0:T(512)(128)(4,1)S(1)}, u32[]{:S(2)}) copy-start(pred[8]{0:T(512)(128)(4,1)S(1)} %get-tuple-element.124) | copy-start | bytes 28
  11.2 43.9 %collective-permute-start.2 = (bf16[2,32,512]{2,1,0:T(8,128)(2,1)}, bf16[2,32,512]{2,1,0:T(8,128)(2,1)S(1)}, u32[]{:S(2)}, u32[]{:S(2)}) collective-permute-start(bf16[2,32,512]{2,1,0:T(8,128)(2,1)} %copy.145), channel_id=1, source_target_pairs={{0,3},{1,0},{2,1},{3,2},{4,7},{5,4},{6,5},{7,6},{8,11},{9,8},{10,9... | collective-permute-start | bytes 196616 | tf_op jit(solution)/shard_map/ppermute | solution.py:19
  14.0 26.3 %collective-permute-start = (bf16[2,32,512]{2,1,0:T(8,128)(2,1)}, bf16[2,32,512]{2,1,0:T(8,128)(2,1)S(1)}, u32[]{:S(2)}, u32[]{:S(2)}) collective-permute-start(bf16[2,32,512]{2,1,0:T(8,128)(2,1)} %copy.145), channel_id=1, source_target_pairs={{0,1},{1,2},{2,3},{3,0},{4,5},{5,6},{6,7},{7,4},{8,9},{9,10},{10,1... | collective-permute-start | bytes 196616 | tf_op jit(solution)/shard_map/ppermute | solution.py:17
  15.3 3.2 copy-start.19
  17.6 1.8 copy-start.31
  17.6 3.0 copy-start.13
  17.6 3.7 %copy-start.11 = (bf16[8,4,512]{2,1,0:T(4,128)(2,1)S(1)}, bf16[8,4,512]{2,1,0:T(4,128)(2,1)}, u32[]{:S(2)}) copy-start(bf16[8,4,512]{2,1,0:T(4,128)(2,1)} %param.23) | copy-start | bytes 98308
  17.7 16.0 %copy-start.4 = (f32[2048]{0:T(1024)S(1)}, f32[2048]{0:T(1024)}, u32[]{:S(2)}) copy-start(f32[2048]{0:T(1024)} %param.30) | copy-start | bytes 24580
  17.7 16.1 %copy-start.32 = (s32[8]{0:T(128)S(1)}, s32[8]{0:T(128)}, u32[]{:S(2)}) copy-start(s32[8]{0:T(128)} %param.24) | copy-start | bytes 100
  17.7 16.7 %copy-start.29 = (f32[256]{0:T(256)S(1)}, f32[256]{0:T(256)}, u32[]{:S(2)}) copy-start(f32[256]{0:T(256)} %param.39) | copy-start | bytes 3076
  18.5 18.9 %copy-start.3 = (bf16[2048,256]{1,0:T(8,128)(2,1)S(1)}, bf16[2048,256]{1,0:T(8,128)(2,1)}, u32[]{:S(2)}) copy-start(bf16[2048,256]{1,0:T(8,128)(2,1)} %param.34) | copy-start | bytes 3145732
  19.4 26.5 %collective-permute-start.3 = (f32[8,17408]{1,0:T(8,128)}, f32[8,17408]{1,0:T(8,128)}, u32[]{:S(2)}, u32[]{:S(2)}) collective-permute-start(f32[8,17408]{1,0:T(8,128)} %broadcast_select_fusion), channel_id=1, source_target_pairs={{0,252},{4,0},{8,4},{12,8},{16,12},{20,16},{24,20},{28,24},{32,28}... | collective-permute-start | bytes 1671176 | tf_op jit(solution)/shard_map/ppermute | solution.py:27
  37.4 36.7 %copy-start.22 = (pred[8]{0:T(512)(128)(4,1)S(1)}, pred[8]{0:T(512)(128)(4,1)}, u32[]{:S(2)}) copy-start(pred[8]{0:T(512)(128)(4,1)} %get-tuple-element.126) | copy-start | bytes 28
  40.3 71.1 %copy-start.1 = (bf16[2048,256]{0,1:T(8,128)(2,1)}, bf16[2048,256]{0,1:T(8,128)(2,1)S(1)}, u32[]{:S(2)}) copy-start(bf16[2048,256]{0,1:T(8,128)(2,1)S(1)} %copy.81) | copy-start | bytes 3145732
  40.3 5.6 %collective-permute-start.1 = (bf16[2,32,512]{2,1,0:T(8,128)(2,1)S(1)}, bf16[2,32,512]{2,1,0:T(8,128)(2,1)S(1)}, u32[]{:S(2)}, u32[]{:S(2)}) collective-permute-start(bf16[2,32,512]{2,1,0:T(8,128)(2,1)S(1)} %collective-permute-done), channel_id=1, source_target_pairs={{0,1},{1,2},{2,3},{3,0},{4,5},{5,6},{6,7},{7,4},{8,9},{9,10},{10,1... | collective-permute-start | bytes 196616 | tf_op jit(solution)/shard_map/ppermute | solution.py:17
  43.1 62.7 %copy-start.21 = (pred[8]{0:T(512)(128)(4,1)S(1)}, pred[8]{0:T(512)(128)(4,1)}, u32[]{:S(2)}) copy-start(pred[8]{0:T(512)(128)(4,1)} %get-tuple-element.128) | copy-start | bytes 28
  47.1 27.0 %collective-permute-start.4 = (f32[8,17408]{1,0:T(8,128)S(1)}, f32[8,17408]{1,0:T(8,128)S(1)}, u32[]{:S(2)}, u32[]{:S(2)}) collective-permute-start(f32[8,17408]{1,0:T(8,128)S(1)} %broadcast_select_fusion.1), channel_id=1, source_target_pairs={{0,248},{4,252},{8,0},{12,4},{16,8},{20,12},{24,16},{28,20},{32,24... | collective-permute-start | bytes 1671176 | tf_op jit(solution)/shard_map/ppermute | solution.py:27
  74.2 11.3 %collective-permute-start.5 = (f32[8,17408]{1,0:T(8,128)S(1)}, f32[8,17408]{1,0:T(8,128)S(1)}, u32[]{:S(2)}, u32[]{:S(2)}) collective-permute-start(f32[8,17408]{1,0:T(8,128)S(1)} %broadcast_select_fusion.2), channel_id=1, source_target_pairs={{0,240},{4,244},{8,248},{12,252},{16,0},{20,4},{24,8},{28,12},{32,... | collective-permute-start | bytes 1671176 | tf_op jit(solution)/shard_map/ppermute | solution.py:27
  74.3 31.6 %copy-start.2 = (bf16[2,32,4096]{2,1,0:T(8,128)(2,1)}, bf16[2,32,4096]{2,1,0:T(8,128)(2,1)S(1)}, u32[]{:S(2)}) copy-start(bf16[2,32,4096]{2,1,0:T(8,128)(2,1)S(1)} %constant_dynamic-update-slice_fusion) | copy-start | bytes 1572868
  86.3 19.6 %collective-permute-start.6 = (f32[8,17408]{1,0:T(8,128)S(1)}, f32[8,17408]{1,0:T(8,128)S(1)}, u32[]{:S(2)}, u32[]{:S(2)}) collective-permute-start(f32[8,17408]{1,0:T(8,128)S(1)} %broadcast_select_fusion.3), channel_id=1, source_target_pairs={{0,224},{4,228},{8,232},{12,236},{16,240},{20,244},{24,248},{28,25... | collective-permute-start | bytes 1671176 | tf_op jit(solution)/shard_map/ppermute | solution.py:27
  86.4 19.7 %copy-start.20 = (f32[2,32]{1,0:T(2,128)}, f32[2,32]{1,0:T(2,128)S(1)}, u32[]{:S(2)}) copy-start(f32[2,32]{1,0:T(2,128)S(1)} %add_rsqrt_fusion.3) | copy-start | bytes 772
  106.0 28.4 %collective-permute-start.7 = (f32[8,17408]{1,0:T(8,128)S(1)}, f32[8,17408]{1,0:T(8,128)}, u32[]{:S(2)}, u32[]{:S(2)}) collective-permute-start(f32[8,17408]{1,0:T(8,128)S(1)} %broadcast_select_fusion.4), channel_id=1, source_target_pairs={{0,192},{4,196},{8,200},{12,204},{16,208},{20,212},{24,216},{28,22... | collective-permute-start | bytes 1671176 | tf_op jit(solution)/shard_map/ppermute | solution.py:27
  134.4 59.9 %copy-start.26 = (pred[8]{0:T(512)(128)(4,1)S(1)}, pred[8]{0:T(512)(128)(4,1)}, u32[]{:S(2)}) copy-start(pred[8]{0:T(512)(128)(4,1)} %get-tuple-element.89) | copy-start | bytes 28
  135.6 58.7 %collective-permute-start.8 = (f32[8,17408]{1,0:T(8,128)S(1)}, f32[8,17408]{1,0:T(8,128)}, u32[]{:S(2)}, u32[]{:S(2)}) collective-permute-start(f32[8,17408]{1,0:T(8,128)S(1)} %broadcast_select_fusion.5), channel_id=1, source_target_pairs={{0,128},{4,132},{8,136},{12,140},{16,144},{20,148},{24,152},{28,15... | collective-permute-start | bytes 1671176 | tf_op jit(solution)/shard_map/ppermute | solution.py:27
  135.7 77.4 %copy-start.15 = (pred[8]{0:T(512)(128)(4,1)S(1)}, pred[8]{0:T(512)(128)(4,1)}, u32[]{:S(2)}) copy-start(pred[8]{0:T(512)(128)(4,1)} %copy-done.14) | copy-start | bytes 28
  135.7 77.4 %copy-start.18 = (pred[8]{0:T(512)(128)(4,1)S(1)}, pred[8]{0:T(512)(128)(4,1)}, u32[]{:S(2)}) copy-start(pred[8]{0:T(512)(128)(4,1)} %get-tuple-element.86) | copy-start | bytes 28
  192.1 21.2 %copy-start.17 = (f32[1,2048]{1,0:T(1,128)S(1)}, f32[1,2048]{1,0:T(1,128)}, u32[]{:S(2)}) copy-start(f32[1,2048]{1,0:T(1,128)} %get-tuple-element.101) | copy-start | bytes 24580
  193.0 21.6 %copy-start.12 = (bf16[64,256]{1,0:T(8,128)(2,1)S(1)}, bf16[64,256]{1,0:T(8,128)(2,1)}, u32[]{:S(2)}) copy-start(bf16[64,256]{1,0:T(8,128)(2,1)} %param.37) | copy-start | bytes 98308
  193.1 21.6 %copy-start.27 = (f32[256]{0:T(256)S(1)}, f32[256]{0:T(256)}, u32[]{:S(2)}) copy-start(f32[256]{0:T(256)} %param.38) | copy-start | bytes 3076
  218.1 5.9 %copy-start.5 = (f32[8,4,64]{2,1,0:T(4,128)S(1)}, f32[8,4,64]{2,1,0:T(4,128)}, u32[]{:S(2)}) copy-start(f32[8,4,64]{2,1,0:T(4,128)} %get-tuple-element.111) | copy-start | bytes 24580
  218.1 5.9 %copy-start.6 = (f32[8,4,64]{2,1,0:T(4,128)S(1)}, f32[8,4,64]{2,1,0:T(4,128)}, u32[]{:S(2)}) copy-start(f32[8,4,64]{2,1,0:T(4,128)} %get-tuple-element.108) | copy-start | bytes 24580
  218.1 5.9 %copy-start.7 = (f32[8,4,64]{2,1,0:T(4,128)S(1)}, f32[8,4,64]{2,1,0:T(4,128)}, u32[]{:S(2)}) copy-start(f32[8,4,64]{2,1,0:T(4,128)} %get-tuple-element.110) | copy-start | bytes 24580
  218.1 5.9 %copy-start.8 = (f32[8,4,64]{2,1,0:T(4,128)S(1)}, f32[8,4,64]{2,1,0:T(4,128)}, u32[]{:S(2)}) copy-start(f32[8,4,64]{2,1,0:T(4,128)} %get-tuple-element.109) | copy-start | bytes 24580
  220.1 8.0 %copy-start.16 = (f32[4,64]{1,0:T(4,128)S(1)}, f32[4,64]{1,0:T(4,128)}, u32[]{:S(2)}) copy-start(f32[4,64]{1,0:T(4,128)} %mul.349) | copy-start | bytes 3076
  220.1 8.0 %copy-start.23 = (pred[8]{0:T(512)(128)(4,1)S(1)}, pred[8]{0:T(512)(128)(4,1)}, u32[]{:S(2)}) copy-start(pred[8]{0:T(512)(128)(4,1)} %get-tuple-element.133) | copy-start | bytes 28
  220.1 8.0 %copy-start.24 = (pred[8]{0:T(512)(128)(4,1)S(1)}, pred[8]{0:T(512)(128)(4,1)}, u32[]{:S(2)}) copy-start(pred[8]{0:T(512)(128)(4,1)} %get-tuple-element.135) | copy-start | bytes 28
  220.1 8.0 %copy-start.25 = (pred[8]{0:T(512)(128)(4,1)S(1)}, pred[8]{0:T(512)(128)(4,1)}, u32[]{:S(2)}) copy-start(pred[8]{0:T(512)(128)(4,1)} %get-tuple-element.134) | copy-start | bytes 28
  231.0 5.8 %copy-start.30 = (f32[256]{0:T(256)S(1)}, f32[256]{0:T(256)}, u32[]{:S(2)}) copy-start(f32[256]{0:T(256)} %param.40) | copy-start | bytes 3076
  233.2 4.9 %copy-start.33 = (s32[8]{0:T(128)S(1)}, s32[8]{0:T(128)}, u32[]{:S(2)}) copy-start(s32[8]{0:T(128)} %broadcast_add_fusion) | copy-start | bytes 100
  233.2 56.4 %copy-start.9 = (f32[2048]{0:T(1024)S(1)}, f32[2048]{0:T(1024)}, u32[]{:S(2)}) copy-start(f32[2048]{0:T(1024)} %param.31) | copy-start | bytes 24580
  233.2 56.6 %copy-start.10 = (f32[1,2048]{1,0:T(1,128)S(1)}, f32[1,2048]{1,0:T(1,128)}, u32[]{:S(2)}) copy-start(f32[1,2048]{1,0:T(1,128)} %get-tuple-element.99) | copy-start | bytes 24580
  237.8 82.5 %reduce-scatter.2.cloned.1.call-start = ((), (), s32[]{:S(2)}) async-start(), calls=%async_computation.2 | async-start | bytes 163840 | tf_op jit(solution)/shard_map/reduce_scatter | solution.py:302
  293.2 27.9 %copy-start.28 = (pred[8,4]{1,0:T(8,128)(4,1)S(1)}, pred[8,4]{1,0:T(8,128)(4,1)}, u32[]{:S(2)}) copy-start(pred[8,4]{1,0:T(8,128)(4,1)} %iota_compare_fusion.1) | copy-start | bytes 100
Sparse Core Ops, SparseCore 0:
  237.9 50.3 all-reduce.2
  296.9 23.3 reduce-scatter.1
